TPU v7x, 32 devices: a whole 2x2x4 slice. The times are simulated.
32 devices in a mesh: vocab: 4 (over z), expert: 8 (over y, x, core).
Axes of the slice: x: 2, y: 2, z: 4, core: 2. Of those that a mesh axis runs over, the one named last changes fastest.
Arguments:
- token_ids: int32 [1024], replicated, may hold values from 0 to 75967
- word_mask: int32 [75968], P('vocab'), may hold values 0 or 1
- embed_table: bfloat16 [75968, 4096], P('vocab', 'expert'), may hold values from -6 to 6
- attn_out: bfloat16 [1024, 4096], P('expert', 'vocab'), may hold values from -6 to 6
- in_gain: float32 [4096], replicated, may hold values from 0.25 to 1.75
- key_weight: bfloat16 [4096, 512], P(None, 'vocab'), may hold values from -0.09375 to 0.09375
- key_gain: float32 [128], replicated, may hold values from 0.25 to 1.75
- post_gain: float32 [4096], replicated, may hold values from 0.25 to 1.75
- routes: int32 [1024, 8], P('expert'), may hold values from 0 to 15, all different within a row; in each aligned block of 128 rows (0 to 127, 128 to 255, ...) at most 96 rows name the same one
- gate_ints: int32 [1024, 8], P('expert'), may hold values from 1 to 63
- w_gate: bfloat16 [32, 4096, 768], P(('expert', 'vocab')), may hold values from -0.09375 to 0.09375
- w_up: bfloat16 [32, 4096, 768], P(('expert', 'vocab')), may hold values from -0.09375 to 0.09375
- w_down: bfloat16 [32, 768, 4096], P(('expert', 'vocab')), may hold values from -0.15625 to 0.15625
Outputs:
- expert_out: bfloat16 [1024, 4096], P('expert', 'vocab')
- key_heads: bfloat16 [1024, 512], P('expert', 'vocab')
Inputs may be any that keep to these rules, and one draw needn't show every extreme that they name: `routes`: each row names 8 different experts; within the 128 rows of one index of expert no expert is named by more than 96 rows, and in some such blocks one is named by exactly 96.
All inputs are finite; a program needn't handle non-finite values. No bound on the sum of `word_mask` on one device may be relied on, other than what follows from the above.
Results may differ from a plain program's by a relative error of at most 0.008.
Values may be sent and summed in bfloat16 or wider, within the bound.
A program may use at most 192 MiB of HBM per device.

v0:
```python
import jax
import jax.numpy as jnp
from jax import lax
from jax.sharding import PartitionSpec as P


def rms_rows(values, scale_gain):
    inverse_rms = lax.rsqrt(jnp.mean(values * values, axis=-1, keepdims=True) + 1e-06)
    return values * inverse_rms * scale_gain


def on_device(
    token_ids,
    word_mask,
    embed_table,
    attn_out,
    in_gain,
    key_weight,
    key_gain,
    post_gain,
    routes,
    gate_ints,
    w_gate,
    w_up,
    w_down,
):
    n_vocab = lax.axis_size("vocab")
    n_expert = lax.axis_size("expert")
    vocab_rows = embed_table.shape[0]
    experts_total = n_expert * n_vocab // 2
    whole_mesh = ("expert", "vocab")
    my_vocab = lax.axis_index("vocab")
    my_expert = (lax.axis_index("expert") * n_vocab + my_vocab) // 2
    gate_share = gate_ints.astype(jnp.float32) / jnp.sum(gate_ints, axis=1, keepdims=True).astype(
        jnp.float32
    )
    onehot = routes[:, :, None] == jnp.arange(experts_total, dtype=jnp.int32)[None, None, :]
    share_of = jnp.sum(jnp.where(onehot, gate_share[:, :, None], 0.0), axis=1)
    all_shares = lax.all_gather(share_of, "expert", axis=0, tiled=True)
    my_share = lax.dynamic_slice_in_dim(all_shares, my_expert, 1, axis=1)
    own_rows = attn_out.shape[0] // n_vocab
    attn_full = lax.all_gather(attn_out, "vocab", axis=1, tiled=True)
    attn_rows = lax.dynamic_slice_in_dim(attn_full, my_vocab * own_rows, own_rows, axis=0)
    local_ids = token_ids - my_vocab * vocab_rows
    inside = (local_ids >= 0) & (local_ids < vocab_rows)
    safe_ids = jnp.clip(local_ids, 0, vocab_rows - 1)
    keep_row = inside & (word_mask[safe_ids] == 1)
    partial_value = jnp.where(
        keep_row[:, None], embed_table[safe_ids], jnp.zeros_like(embed_table[:1])
    )
    moved_rows = lax.all_to_all(partial_value, "expert", split_axis=0, concat_axis=1, tiled=True)
    rows = lax.psum_scatter(moved_rows, "vocab", scatter_dimension=0, tiled=True)
    rows = rows.astype(jnp.float32)
    mid_rows = (rows + attn_rows.astype(jnp.float32)).astype(jnp.bfloat16)
    expert_in = rms_rows(mid_rows.astype(jnp.float32), post_gain).astype(jnp.bfloat16)
    tokens_in = lax.all_gather(expert_in, whole_mesh, axis=0, tiled=True)
    normed_rows = rms_rows(rows, in_gain).astype(jnp.bfloat16)
    tokens_in, normed_rows = lax.optimization_barrier((tokens_in, normed_rows))
    key_rows = lax.all_gather(normed_rows, "vocab", axis=0, tiled=True)
    gate_val = jnp.dot(tokens_in, w_gate[0], preferred_element_type=jnp.float32)
    up_val = jnp.dot(tokens_in, w_up[0], preferred_element_type=jnp.float32)
    hidden = (jax.nn.silu(gate_val) * up_val).astype(jnp.bfloat16)
    parts = jnp.dot(hidden, w_down[0], preferred_element_type=jnp.float32)
    weighted = (parts * my_share).astype(jnp.bfloat16)
    weighted, key_rows = lax.optimization_barrier((weighted, key_rows))
    raw_keys = jnp.dot(key_rows, key_weight, preferred_element_type=jnp.float32)
    key_heads = rms_rows(raw_keys, key_gain).astype(jnp.bfloat16)
    by_tokens = lax.psum_scatter(weighted, "expert", scatter_dimension=0, tiled=True)
    expert_out = lax.psum_scatter(by_tokens, "vocab", scatter_dimension=1, tiled=True)
    return (expert_out, key_heads)


def solution(mesh):
    return jax.shard_map(
        on_device,
        mesh=mesh,
        in_specs=(
            P(),
            P("vocab"),
            P("vocab", "expert"),
            P("expert", "vocab"),
            P(),
            P(None, "vocab"),
            P(),
            P(),
            P("expert", None),
            P("expert", None),
            P(("expert", "vocab"), None, None),
            P(("expert", "vocab"), None, None),
            P(("expert", "vocab"), None, None),
        ),
        out_specs=(P("expert", "vocab"), P("expert", "vocab")),
        check_vma=False,
    )
```

profile of v0, /device:TPU:0, one launch (start us, length us, event | category | flops | bytes accessed | tf_op | source)
XLA Modules:
  0.0 295.7 jit_solution(1607068945751043418)
XLA Ops:
  7.2 0.0 copy-start
  7.2 0.0 all-gather.4.cloned.1.call-start
  7.2 0.7 all-gather.4.cloned.1.call-update
  7.9 0.0 reduce-scatter.4.cloned.1.call-start
  8.0 0.7 fusion.14
  8.7 5.9 %gather_fusion = s32[1024]{0:T(1024)S(1)} fusion(s32[18992]{0:T(1024)} %param.14, s32[1024]{0:T(1024)S(1)} %fusion.14), kind=kCustom, calls=%fused_computation | custom fusion | bytes 12288 | tf_op jit(solution)/shard_map/gather | solution.py:47
  14.6 13.3 %gather_fusion.1 = bf16[1024,512]{1,0:T(8,128)(2,1)S(1)} fusion(bf16[18992,512]{1,0:T(8,128)(2,1)} %param.15, s32[1024]{0:T(1024)S(1)} %fusion.14), kind=kCustom, calls=%fused_computation.1 | custom fusion | bytes 2101248 | tf_op jit(solution)/shard_map/gather | solution.py:49
  27.9 0.0 copy-done.5
  27.9 0.0 copy-start.2
  27.9 0.0 copy-start.3
  27.9 0.0 copy-start.4
  28.0 0.0 copy-start.6
  28.0 0.2 broadcast_select_fusion
  28.2 20.3 %all_to_all.16 = bf16[8,128,512]{2,1,0:T(8,128)(2,1)S(1)} all-to-all(bf16[8,128,512]{2,1,0:T(8,128)(2,1)S(1)} %broadcast_select_fusion), channel_id=1, replica_groups=mesh['vocab'=4,'expert'=8] {'expert'}, dimensions={0} | all-to-all | bytes 2097152 | tf_op jit(solution)/shard_map/all_to_all | solution.py:51
  48.5 1.1 copy.25
  49.6 0.0 reduce-scatter.4.cloned.1.call-update
  49.7 0.0 all-gather.6.cloned.1.call-start
  49.7 0.0 all-gather.4.cloned.1.call-done
  49.7 26.6 %reduce-scatter.4.cloned.1.call-done = bf16[32,4096]{1,0:T(8,128)(2,1)} async-done(((bf16[128,4096]{1,0:T(8,128)(2,1)}), bf16[32,4096]{1,0:T(8,128)(2,1)}) %reduce-scatter.4.cloned.1.call-update) | async-done | bytes 262160 | tf_op jit(solution)/shard_map/reduce_scatter | solution.py:52
  76.3 1.3 fusion.11
  77.6 0.0 copy-done.2
  77.6 0.0 copy-done.3
  77.6 2.0 fusion.13
  79.6 0.0 all-gather.6.cloned.1.call-update
  79.7 0.0 all-gather.8.cloned.1.call-start
  79.7 0.0 copy-done.4
  79.8 0.0 copy-done.6
  79.8 9.0 %all_gather.14 = f32[1024,16]{0,1:T(8,128)S(1)} all-gather(f32[128,16]{0,1:T(8,128)S(1)} %select_reduce_fusion), channel_id=1, replica_groups=mesh['vocab'=4,'expert'=8] {'expert'}, dimensions={0}, use_global_device_ids=true | all-gather | bytes 73728 | tf_op jit(solution)/shard_map/all_gather | solution.py:39
  88.9 67.0 %all-gather.6.cloned.1.call-done = bf16[1024,4096]{1,0:T(8,128)(2,1)} async-done(((bf16[32,4096]{1,0:T(8,128)(2,1)}), bf16[1024,4096]{1,0:T(8,128)(2,1)}) %all-gather.6.cloned.1.call-update) | async-done | bytes 8388624 | tf_op jit(solution)/shard_map/all_gather | solution.py:56
  155.9 0.0 all-gather.8.cloned.1.call-update
  155.9 0.2 reduce-scatter.6.cloned.1.call-start
  156.1 0.0 copy-start.8
  156.1 0.0 slice-start
  156.2 11.0 %fusion.1 = f32[1024,768]{1,0:T(8,128)S(1)} fusion(bf16[1024,4096]{1,0:T(8,128)(2,1)} %all-gather.6.cloned.1.call-done, bf16[1,4096,768]{2,1,0:T(8,128)(2,1)} %param.24), kind=kOutput, calls=%fused_computation.4 | convolution fusion | flops 6442450944 | bytes 17825792 | tf_op jit(solution)/shard_map/dot_general | solution.py:61
  167.2 0.0 copy-done.8
  167.2 0.0 slice-start.1
  167.2 10.0 %multiply_convert_fusion.1 = bf16[1024,768]{1,0:T(8,128)(2,1)S(1)} fusion(f32[1024,768]{1,0:T(8,128)S(1)} %fusion.1, bf16[1024,4096]{1,0:T(8,128)(2,1)S(1)} %copy-done.8, bf16[1,4096,768]{2,1,0:T(8,128)(2,1)} %param.23), kind=kOutput, calls=%fused_computation.8 | convolution fusion | flops 6447169536 | bytes 19398656 | tf_op jit(solution)/shard_map/dot_general | solution.py:60
  177.2 0.0 slice-done
  177.2 0.0 slice-done.1
  177.2 8.9 %multiply_convert_fusion = bf16[1024,4096]{1,0:T(8,128)(2,1)} fusion(f32[1024]{0:T(1024)S(1)} %bitcast.26, bf16[1024,768]{1,0:T(8,128)(2,1)S(1)} %multiply_convert_fusion.1, bf16[1,768,4096]{2,1,0:T(8,128)(2,1)S(1)} %bitcast.28), kind=kOutput, calls=%fused_computation.2 | convolution fusion | flops 6450839552 | bytes 16257024 | tf_op jit(solution)/shard_map/dot_general | solution.py:63
  186.1 0.0 reduce-scatter.6.cloned.1.call-update
  186.1 0.0 reduce-scatter.8.cloned.1.call-start
  186.2 72.9 %reduce-scatter.6.cloned.1.call-done = bf16[128,4096]{1,0:T(8,128)(2,1)} async-done(((bf16[1024,4096]{1,0:T(8,128)(2,1)}), bf16[128,4096]{1,0:T(8,128)(2,1)}) %reduce-scatter.6.cloned.1.call-update) | async-done | bytes 1048592 | tf_op jit(solution)/shard_map/reduce_scatter | solution.py:68
  259.0 0.0 reduce-scatter.8.cloned.1.call-update
  259.1 0.6 multiply_reduce_fusion
  259.6 0.1 multiply_convert_fusion.2
  259.7 0.7 copy.24
  260.5 28.4 %reduce-scatter.8.cloned.1.call-done = bf16[128,1024]{1,0:T(8,128)(2,1)} async-done(((bf16[128,4096]{1,0:T(8,128)(2,1)}), bf16[128,1024]{1,0:T(8,128)(2,1)}) %reduce-scatter.8.cloned.1.call-update) | async-done | bytes 262160 | tf_op jit(solution)/shard_map/reduce_scatter | solution.py:69
  (16 shorter events, 0.1 us)
Async XLA Ops:
  7.2 251.9 %copy-start = (bf16[4096,128]{1,0:T(8,128)(2,1)S(1)}, bf16[4096,128]{1,0:T(8,128)(2,1)}, u32[]{:S(2)}) copy-start(bf16[4096,128]{1,0:T(8,128)(2,1)} %param.18) | copy-start | bytes 3145732
  7.2 42.6 %all-gather.4.cloned.1.call-start = ((), (), s32[]{:S(2)}) async-start(), calls=%async_computation.5 | async-start | bytes 1310720 | tf_op jit(solution)/shard_map/all_gather | solution.py:42
  7.9 68.4 %reduce-scatter.4.cloned.1.call-start = ((), (), s32[]{:S(2)}) async-start(), calls=%async_computation.4 | async-start | bytes 1310720 | tf_op jit(solution)/shard_map/reduce_scatter | solution.py:52
  8.7 19.2 %copy-start.5 = (s32[1024]{0:T(1024)S(1)}, s32[1024]{0:T(1024)}, u32[]{:S(2)}) copy-start(s32[1024]{0:T(1024)} %param.13) | copy-start | bytes 12292
  27.9 49.7 %copy-start.2 = (f32[4096]{0:T(1024)S(1)}, f32[4096]{0:T(1024)}, u32[]{:S(2)}) copy-start(f32[4096]{0:T(1024)} %param.17) | copy-start | bytes 49156
  27.9 49.7 %copy-start.3 = (f32[4096]{0:T(1024)S(1)}, f32[4096]{0:T(1024)}, u32[]{:S(2)}) copy-start(f32[4096]{0:T(1024)} %param.20) | copy-start | bytes 49156
  27.9 51.8 %copy-start.4 = (s32[128,8]{0,1:T(8,128)S(1)}, s32[128,8]{0,1:T(8,128)}, u32[]{:S(2)}) copy-start(s32[128,8]{0,1:T(8,128)} %param.22) | copy-start | bytes 12292
  28.0 51.8 %copy-start.6 = (s32[128,8]{0,1:T(8,128)S(1)}, s32[128,8]{0,1:T(8,128)}, u32[]{:S(2)}) copy-start(s32[128,8]{0,1:T(8,128)} %param.21) | copy-start | bytes 12292
  49.7 106.2 %all-gather.6.cloned.1.call-start = ((), (), s32[]{:S(2)}) async-start(), calls=%async_computation.6 | async-start | bytes 8650752 | tf_op jit(solution)/shard_map/all_gather | solution.py:56
  79.7 106.4 %all-gather.8.cloned.1.call-start = ((), (), s32[]{:S(2)}) async-start(), calls=%async_computation.7 | async-start | bytes 1310720 | tf_op jit(solution)/shard_map/all_gather | solution.py:59
  155.9 103.1 %reduce-scatter.6.cloned.1.call-start = ((), (), s32[]{:S(2)}) async-start(), calls=%async_computation.8 | async-start | bytes 9437184 | tf_op jit(solution)/shard_map/reduce_scatter | solution.py:68
  156.1 11.1 %copy-start.8 = (bf16[1024,4096]{1,0:T(8,128)(2,1)S(1)}, bf16[1024,4096]{1,0:T(8,128)(2,1)}, u32[]{:S(2)}) copy-start(bf16[1024,4096]{1,0:T(8,128)(2,1)} %all-gather.6.cloned.1.call-done) | copy-start | bytes 25165828
  156.1 21.0 %slice-start = ((s8[6291456]{0:T(1024)(128)(4,1)}), s8[4194304]{0:T(1024)(128)(4,1)S(1)}, s32[]{:S(2)}) async-start(s8[6291456]{0:T(1024)(128)(4,1)} %bitcast.27), calls=%async_computation.10 | async-start | bytes 8388608
  167.2 10.0 %slice-start.1 = ((s8[6291456]{0:T(1024)(128)(4,1)}), s8[2097152]{0:T(1024)(128)(4,1)S(1)}, s32[]{:S(2)}) async-start(s8[6291456]{0:T(1024)(128)(4,1)} %bitcast.27), calls=%async_computation.11 | async-start | bytes 4194304
  186.1 73.5 %copy-start.7 = (f32[128]{0:T(128)S(1)}, f32[128]{0:T(128)}, u32[]{:S(2)}) copy-start(f32[128]{0:T(128)} %param.19) | copy-start | bytes 1540
  186.1 73.0 %copy-start.1 = (bf16[128,4096]{1,0:T(8,128)(2,1)S(1)}, bf16[128,4096]{1,0:T(8,128)(2,1)}, u32[]{:S(2)}) copy-start(bf16[128,4096]{1,0:T(8,128)(2,1)} %all-gather.8.cloned.1.call-done) | copy-start | bytes 3145732
  186.1 102.8 %reduce-scatter.8.cloned.1.call-start = ((), (), s32[]{:S(2)}) async-start(), calls=%async_computation.9 | async-start | bytes 1310720 | tf_op jit(solution)/shard_map/reduce_scatter | solution.py:69
Sparse Core Ops, SparseCore 0:
  9.6 30.6 all-gather.3
  49.8 26.4 reduce-scatter.3
  79.8 76.0 all-gather.5
  158.0 26.5 all-gather.7
  188.2 70.7 reduce-scatter.5
  261.7 27.1 reduce-scatter.7
where the time goes:
time: 296 us
  waiting for transfers between devices  196 us (66%)
  matrix products  30.4 us (10%)
  blocking collectives  29.4 us (10%)
  local copies, waits for them, and re-layouts  21.1 us (7%)
  between operations  14.4 us (5%)
  other arithmetic  4.34 us (1%)
    reduce_scatter x1, waiting for transfers between devices, on_device(): lax.psum_scatter(weighted, 'expert', scatter_dimension=0, tiled=True)  72.9 us
    all_gather x1, waiting for transfers between devices, on_device(): tokens_in = lax.all_gather(expert_in, whole_mesh, axis=0, tiled=True)  67 us
    reduce_scatter x1, waiting for transfers between devices, on_device(): lax.psum_scatter(by_tokens, 'vocab', scatter_dimension=1, tiled=True)  28.4 us
    reduce_scatter x1, waiting for transfers between devices, on_device(): lax.psum_scatter(moved_rows, 'vocab', scatter_dimension=0, tiled=True)  26.6 us
    all_to_all x1, blocking collectives, on_device(): lax.all_to_all(partial_value, 'expert', split_axis=0, concat_axis=1, tile...  20.3 us
    gather x1, local copies, waits for them, and re-layouts, on_device(): embed_table[safe_ids]  13.3 us
    dot_general x1, matrix products, on_device(): up_val = jnp.dot(tokens_in, w_up[0], preferred_element_type=jnp.float32)  11 us
    dot_general x1, matrix products, on_device(): gate_val = jnp.dot(tokens_in, w_gate[0], preferred_element_type=jnp.float32)  9.95 us
  transfers between devices with their start and end apart: 6, of which 4 were waited for; matrix products, arithmetic and copies ran while one was open for 18% of the time, Pallas kernels for 0%

commit v1 on v0

--- a/solution.py
+++ b/solution.py
@@ -36,7 +36,14 @@
     )
     onehot = routes[:, :, None] == jnp.arange(experts_total, dtype=jnp.int32)[None, None, :]
     share_of = jnp.sum(jnp.where(onehot, gate_share[:, :, None], 0.0), axis=1)
-    all_shares = lax.all_gather(share_of, "expert", axis=0, tiled=True)
+    ring = [share_of]
+    for hop in range(7):
+        ring.append(lax.ppermute(ring[-1], "expert", [(dev, (dev + 1) % 8) for dev in range(8)]))
+    all_shares = jnp.roll(
+        jnp.concatenate(ring[::-1], axis=0),
+        (lax.axis_index("expert") + 1) * ring[0].shape[0],
+        axis=0,
+    )
     my_share = lax.dynamic_slice_in_dim(all_shares, my_expert, 1, axis=1)
     own_rows = attn_out.shape[0] // n_vocab
     attn_full = lax.all_gather(attn_out, "vocab", axis=1, tiled=True)

time: 296 us -> 296 us (level)
  blocking collectives: 29.4 us -> 20.3 us
  waiting for transfers between devices: 196 us -> 204 us
    ppermute x0 -> x7, waiting for transfers between devices: none -> 27.9 us  [on_device(): lax.ppermute(ring[-1], 'expert', [(dev, (dev + 1) % 8) for dev in range(8)])]
    all_gather x1, waiting for transfers between devices: 67 us -> 47.8 us  [on_device(): tokens_in = lax.all_gather(expert_in, whole_mesh, axis=0, tiled=True)]
    all_gather x1 -> x0, blocking collectives: 9.05 us -> none  [on_device(): all_shares = lax.all_gather(share_of, 'expert', axis=0, tiled=True)]
  transfers between devices with their start and end apart: 6 -> 13, of which waited for: 4 -> 11; matrix products, arithmetic and copies ran while one was open for 18% -> 18% of each run, Pallas kernels for 0% -> 0%
where the time goes in v1:
time: 296 us
  waiting for transfers between devices  204 us (69%)
  matrix products  30.6 us (10%)
  local copies, waits for them, and re-layouts  21.3 us (7%)
  blocking collectives  20.3 us (7%)
  between operations  14.5 us (5%)
  other arithmetic  4.34 us (1%)
    reduce_scatter x1, waiting for transfers between devices, on_device(): lax.psum_scatter(weighted, 'expert', scatter_dimension=0, tiled=True)  72.7 us
    all_gather x1, waiting for transfers between devices, on_device(): tokens_in = lax.all_gather(expert_in, whole_mesh, axis=0, tiled=True)  47.8 us
    reduce_scatter x1, waiting for transfers between devices, on_device(): lax.psum_scatter(by_tokens, 'vocab', scatter_dimension=1, tiled=True)  28.4 us
    ppermute x7, waiting for transfers between devices, on_device(): lax.ppermute(ring[-1], 'expert', [(dev, (dev + 1) % 8) for dev in range(8)])  27.9 us
    reduce_scatter x1, waiting for transfers between devices, on_device(): lax.psum_scatter(moved_rows, 'vocab', scatter_dimension=0, tiled=True)  26.6 us
    all_to_all x1, blocking collectives, on_device(): lax.all_to_all(partial_value, 'expert', split_axis=0, concat_axis=1, tile...  20.3 us
    gather x1, local copies, waits for them, and re-layouts, on_device(): embed_table[safe_ids]  13.3 us
    dot_general x1, matrix products, on_device(): up_val = jnp.dot(tokens_in, w_up[0], preferred_element_type=jnp.float32)  11 us
  transfers between devices with their start and end apart: 13, of which 11 were waited for; matrix products, arithmetic and copies ran while one was open for 18% of the time, Pallas kernels for 0%

profile of v1, /device:TPU:0, one launch (start us, length us, event | category | flops | bytes accessed | tf_op | source)
XLA Modules:
  0.0 295.7 jit_solution(14161803342738990744)
XLA Ops:
  7.2 0.0 copy-start
  7.2 0.0 all-gather.4.cloned.1.call-start
  7.2 0.7 all-gather.4.cloned.1.call-update
  7.9 0.0 reduce-scatter.4.cloned.1.call-start
  8.0 0.7 fusion.17
  8.7 5.9 %gather_fusion = s32[1024]{0:T(1024)S(1)} fusion(s32[18992]{0:T(1024)} %param.14, s32[1024]{0:T(1024)S(1)} %fusion.17), kind=kCustom, calls=%fused_computation | custom fusion | bytes 12288 | tf_op jit(solution)/shard_map/gather | solution.py:54
  14.6 13.3 %gather_fusion.1 = bf16[1024,512]{1,0:T(8,128)(2,1)S(1)} fusion(bf16[18992,512]{1,0:T(8,128)(2,1)} %param.15, s32[1024]{0:T(1024)S(1)} %fusion.17), kind=kCustom, calls=%fused_computation.1 | custom fusion | bytes 2101248 | tf_op jit(solution)/shard_map/gather | solution.py:56
  27.9 0.0 copy-start.2
  27.9 0.0 copy-start.3
  27.9 0.0 copy-start.4
  28.0 0.0 copy-start.6
  28.0 0.2 broadcast_select_fusion
  28.2 20.3 %all_to_all.16 = bf16[8,128,512]{2,1,0:T(8,128)(2,1)S(1)} all-to-all(bf16[8,128,512]{2,1,0:T(8,128)(2,1)S(1)} %broadcast_select_fusion), channel_id=1, replica_groups=mesh['vocab'=4,'expert'=8] {'expert'}, dimensions={0} | all-to-all | bytes 2097152 | tf_op jit(solution)/shard_map/all_to_all | solution.py:58
  48.5 1.1 copy.25
  49.6 0.0 reduce-scatter.4.cloned.1.call-update
  49.7 0.0 all-gather.6.cloned.1.call-start
  49.7 0.0 all-gather.4.cloned.1.call-done
  49.7 26.6 %reduce-scatter.4.cloned.1.call-done = bf16[32,4096]{1,0:T(8,128)(2,1)} async-done(((bf16[128,4096]{1,0:T(8,128)(2,1)}), bf16[32,4096]{1,0:T(8,128)(2,1)}) %reduce-scatter.4.cloned.1.call-update) | async-done | bytes 262160 | tf_op jit(solution)/shard_map/reduce_scatter | solution.py:59
  76.3 1.3 fusion.14
  77.6 2.0 fusion.16
  79.6 0.0 all-gather.6.cloned.1.call-update
  79.7 0.0 all-gather.8.cloned.1.call-start
  79.8 0.1 collective-permute-start
  79.9 4.0 %collective-permute-done = f32[128,16]{0,1:T(8,128)S(1)} collective-permute-done((f32[128,16]{0,1:T(8,128)S(1)}, f32[128,16]{0,1:T(8,128)S(1)}, u32[]{:S(2)}, u32[]{:S(2)}) %collective-permute-start) | collective-permute-done | bytes 8224 | tf_op jit(solution)/shard_map/ppermute | solution.py:41
  83.8 0.0 collective-permute-start.1
  83.8 4.0 %collective-permute-done.1 = f32[128,16]{0,1:T(8,128)S(1)} collective-permute-done((f32[128,16]{0,1:T(8,128)S(1)}, f32[128,16]{0,1:T(8,128)S(1)}, u32[]{:S(2)}, u32[]{:S(2)}) %collective-permute-start.1) | collective-permute-done | bytes 8224 | tf_op jit(solution)/shard_map/ppermute | solution.py:41
  87.8 4.0 %collective-permute-done.2 = f32[128,16]{0,1:T(8,128)S(1)} collective-permute-done((f32[128,16]{0,1:T(8,128)S(1)}, f32[128,16]{0,1:T(8,128)S(1)}, u32[]{:S(2)}, u32[]{:S(2)}) %collective-permute-start.2) | collective-permute-done | bytes 8224 | tf_op jit(solution)/shard_map/ppermute | solution.py:41
  91.8 4.0 %collective-permute-done.3 = f32[128,16]{0,1:T(8,128)S(1)} collective-permute-done((f32[128,16]{0,1:T(8,128)S(1)}, f32[128,16]{0,1:T(8,128)S(1)}, u32[]{:S(2)}, u32[]{:S(2)}) %collective-permute-start.3) | collective-permute-done | bytes 8224 | tf_op jit(solution)/shard_map/ppermute | solution.py:41
  95.8 4.0 %collective-permute-done.4 = f32[128,16]{0,1:T(8,128)S(1)} collective-permute-done((f32[128,16]{0,1:T(8,128)S(1)}, f32[128,16]{0,1:T(8,128)S(1)}, u32[]{:S(2)}, u32[]{:S(2)}) %collective-permute-start.4) | collective-permute-done | bytes 8224 | tf_op jit(solution)/shard_map/ppermute | solution.py:41
  99.8 4.0 %collective-permute-done.5 = f32[128,16]{0,1:T(8,128)S(1)} collective-permute-done((f32[128,16]{0,1:T(8,128)S(1)}, f32[128,16]{0,1:T(8,128)S(1)}, u32[]{:S(2)}, u32[]{:S(2)}) %collective-permute-start.5) | collective-permute-done | bytes 8224 | tf_op jit(solution)/shard_map/ppermute | solution.py:41
  103.7 4.1 %collective-permute-done.6 = f32[128,16]{0,1:T(8,128)S(1)} collective-permute-done((f32[128,16]{0,1:T(8,128)S(1)}, f32[128,16]{0,1:T(8,128)S(1)}, u32[]{:S(2)}, u32[]{:S(2)}) %collective-permute-start.6) | collective-permute-done | bytes 8224 | tf_op jit(solution)/shard_map/ppermute | solution.py:41
  108.0 0.1 dynamic_slice.9
  108.0 47.8 %all-gather.6.cloned.1.call-done = bf16[1024,4096]{1,0:T(8,128)(2,1)} async-done(((bf16[32,4096]{1,0:T(8,128)(2,1)}), bf16[1024,4096]{1,0:T(8,128)(2,1)}) %all-gather.6.cloned.1.call-update) | async-done | bytes 8388624 | tf_op jit(solution)/shard_map/all_gather | solution.py:63
  155.9 0.0 all-gather.8.cloned.1.call-update
  155.9 0.2 reduce-scatter.6.cloned.1.call-start
  156.1 0.0 slice-start
  156.1 11.0 %fusion.4 = f32[1024,768]{1,0:T(8,128)S(1)} fusion(bf16[1024,4096]{1,0:T(8,128)(2,1)} %all-gather.6.cloned.1.call-done, bf16[1,4096,768]{2,1,0:T(8,128)(2,1)} %param.24), kind=kOutput, calls=%fused_computation.5 | convolution fusion | flops 6442450944 | bytes 17825792 | tf_op jit(solution)/shard_map/dot_general | solution.py:68
  167.2 0.0 slice-start.1
  167.2 9.9 %multiply_convert_fusion.1 = bf16[1024,768]{1,0:T(8,128)(2,1)S(1)} fusion(f32[1024,768]{1,0:T(8,128)S(1)} %fusion.4, bf16[1024,4096]{1,0:T(8,128)(2,1)S(1)} %copy-done.8, bf16[1,4096,768]{2,1,0:T(8,128)(2,1)} %param.23), kind=kOutput, calls=%fused_computation.9 | convolution fusion | flops 6447169536 | bytes 19398656 | tf_op jit(solution)/shard_map/dot_general | solution.py:67
  177.2 9.0 %multiply_convert_fusion = bf16[1024,4096]{1,0:T(8,128)(2,1)} fusion(f32[1024]{0:T(1024)S(1)} %bitcast.28, bf16[1024,768]{1,0:T(8,128)(2,1)S(1)} %multiply_convert_fusion.1, bf16[1,768,4096]{2,1,0:T(8,128)(2,1)S(1)} %bitcast.30), kind=kOutput, calls=%fused_computation.2 | convolution fusion | flops 6450839552 | bytes 16257024 | tf_op jit(solution)/shard_map/dot_general | solution.py:70
  186.2 0.0 reduce-scatter.6.cloned.1.call-update
  186.2 0.0 reduce-scatter.8.cloned.1.call-start
  186.3 72.7 %reduce-scatter.6.cloned.1.call-done = bf16[128,4096]{1,0:T(8,128)(2,1)} async-done(((bf16[1024,4096]{1,0:T(8,128)(2,1)}), bf16[128,4096]{1,0:T(8,128)(2,1)}) %reduce-scatter.6.cloned.1.call-update) | async-done | bytes 1048592 | tf_op jit(solution)/shard_map/reduce_scatter | solution.py:75
  259.0 0.0 reduce-scatter.8.cloned.1.call-update
  259.0 0.6 multiply_reduce_fusion
  259.6 0.1 multiply_convert_fusion.2
  259.7 0.7 copy.24
  260.4 28.4 %reduce-scatter.8.cloned.1.call-done = bf16[128,1024]{1,0:T(8,128)(2,1)} async-done(((bf16[128,4096]{1,0:T(8,128)(2,1)}), bf16[128,1024]{1,0:T(8,128)(2,1)}) %reduce-scatter.8.cloned.1.call-update) | async-done | bytes 262160 | tf_op jit(solution)/shard_map/reduce_scatter | solution.py:76
  (45 shorter events, 0.2 us)
Async XLA Ops:
  7.2 251.9 %copy-start = (bf16[4096,128]{1,0:T(8,128)(2,1)S(1)}, bf16[4096,128]{1,0:T(8,128)(2,1)}, u32[]{:S(2)}) copy-start(bf16[4096,128]{1,0:T(8,128)(2,1)} %param.18) | copy-start | bytes 3145732
  7.2 42.6 %all-gather.4.cloned.1.call-start = ((), (), s32[]{:S(2)}) async-start(), calls=%async_computation.5 | async-start | bytes 1310720 | tf_op jit(solution)/shard_map/all_gather | solution.py:49
  7.9 68.4 %reduce-scatter.4.cloned.1.call-start = ((), (), s32[]{:S(2)}) async-start(), calls=%async_computation.4 | async-start | bytes 1310720 | tf_op jit(solution)/shard_map/reduce_scatter | solution.py:59
  8.7 19.2 %copy-start.5 = (s32[1024]{0:T(1024)S(1)}, s32[1024]{0:T(1024)}, u32[]{:S(2)}) copy-start(s32[1024]{0:T(1024)} %param.13) | copy-start | bytes 12292
  27.9 49.7 %copy-start.2 = (f32[4096]{0:T(1024)S(1)}, f32[4096]{0:T(1024)}, u32[]{:S(2)}) copy-start(f32[4096]{0:T(1024)} %param.17) | copy-start | bytes 49156
  27.9 49.7 %copy-start.3 = (f32[4096]{0:T(1024)S(1)}, f32[4096]{0:T(1024)}, u32[]{:S(2)}) copy-start(f32[4096]{0:T(1024)} %param.20) | copy-start | bytes 49156
  27.9 51.8 %copy-start.4 = (s32[128,8]{0,1:T(8,128)S(1)}, s32[128,8]{0,1:T(8,128)}, u32[]{:S(2)}) copy-start(s32[128,8]{0,1:T(8,128)} %param.22) | copy-start | bytes 12292
  28.0 51.8 %copy-start.6 = (s32[128,8]{0,1:T(8,128)S(1)}, s32[128,8]{0,1:T(8,128)}, u32[]{:S(2)}) copy-start(s32[128,8]{0,1:T(8,128)} %param.21) | copy-start | bytes 12292
  49.7 106.2 %all-gather.6.cloned.1.call-start = ((), (), s32[]{:S(2)}) async-start(), calls=%async_computation.6 | async-start | bytes 8650752 | tf_op jit(solution)/shard_map/all_gather | solution.py:63
  79.7 106.6 %all-gather.8.cloned.1.call-start = ((), (), s32[]{:S(2)}) async-start(), calls=%async_computation.7 | async-start | bytes 1310720 | tf_op jit(solution)/shard_map/all_gather | solution.py:66
  79.8 4.0 %collective-permute-start = (f32[128,16]{0,1:T(8,128)S(1)}, f32[128,16]{0,1:T(8,128)S(1)}, u32[]{:S(2)}, u32[]{:S(2)}) collective-permute-start(f32[128,16]{0,1:T(8,128)S(1)} %select_reduce_fusion), channel_id=1, source_target_pairs={{0,1},{1,2},{2,3},{3,4},{4,5},{5,6},{6,7},{7,0},{8,9},{9,10},{10,1... | collective-permute-start | bytes 24584 | tf_op jit(solution)/shard_map/ppermute | solution.py:41
  83.8 4.0 %collective-permute-start.1 = (f32[128,16]{0,1:T(8,128)S(1)}, f32[128,16]{0,1:T(8,128)S(1)}, u32[]{:S(2)}, u32[]{:S(2)}) collective-permute-start(f32[128,16]{0,1:T(8,128)S(1)} %collective-permute-done), channel_id=1, source_target_pairs={{0,1},{1,2},{2,3},{3,4},{4,5},{5,6},{6,7},{7,0},{8,9},{9,10},{10,1... | collective-permute-start | bytes 24584 | tf_op jit(solution)/shard_map/ppermute | solution.py:41
  87.8 4.0 %collective-permute-start.2 = (f32[128,16]{0,1:T(8,128)S(1)}, f32[128,16]{0,1:T(8,128)S(1)}, u32[]{:S(2)}, u32[]{:S(2)}) collective-permute-start(f32[128,16]{0,1:T(8,128)S(1)} %collective-permute-done.1), channel_id=1, source_target_pairs={{0,1},{1,2},{2,3},{3,4},{4,5},{5,6},{6,7},{7,0},{8,9},{9,10},{10,1... | collective-permute-start | bytes 24584 | tf_op jit(solution)/shard_map/ppermute | solution.py:41
  91.8 4.0 %collective-permute-start.3 = (f32[128,16]{0,1:T(8,128)S(1)}, f32[128,16]{0,1:T(8,128)S(1)}, u32[]{:S(2)}, u32[]{:S(2)}) collective-permute-start(f32[128,16]{0,1:T(8,128)S(1)} %collective-permute-done.2), channel_id=1, source_target_pairs={{0,1},{1,2},{2,3},{3,4},{4,5},{5,6},{6,7},{7,0},{8,9},{9,10},{10,1... | collective-permute-start | bytes 24584 | tf_op jit(solution)/shard_map/ppermute | solution.py:41
  95.8 4.0 %collective-permute-start.4 = (f32[128,16]{0,1:T(8,128)S(1)}, f32[128,16]{0,1:T(8,128)S(1)}, u32[]{:S(2)}, u32[]{:S(2)}) collective-permute-start(f32[128,16]{0,1:T(8,128)S(1)} %collective-permute-done.3), channel_id=1, source_target_pairs={{0,1},{1,2},{2,3},{3,4},{4,5},{5,6},{6,7},{7,0},{8,9},{9,10},{10,1... | collective-permute-start | bytes 24584 | tf_op jit(solution)/shard_map/ppermute | solution.py:41
  99.8 4.0 %collective-permute-start.5 = (f32[128,16]{0,1:T(8,128)S(1)}, f32[128,16]{0,1:T(8,128)S(1)}, u32[]{:S(2)}, u32[]{:S(2)}) collective-permute-start(f32[128,16]{0,1:T(8,128)S(1)} %collective-permute-done.4), channel_id=1, source_target_pairs={{0,1},{1,2},{2,3},{3,4},{4,5},{5,6},{6,7},{7,0},{8,9},{9,10},{10,1... | collective-permute-start | bytes 24584 | tf_op jit(solution)/shard_map/ppermute | solution.py:41
  103.7 4.1 %collective-permute-start.6 = (f32[128,16]{0,1:T(8,128)S(1)}, f32[128,16]{0,1:T(8,128)S(1)}, u32[]{:S(2)}, u32[]{:S(2)}) collective-permute-start(f32[128,16]{0,1:T(8,128)S(1)} %collective-permute-done.5), channel_id=1, source_target_pairs={{0,1},{1,2},{2,3},{3,4},{4,5},{5,6},{6,7},{7,0},{8,9},{9,10},{10,1... | collective-permute-start | bytes 24584 | tf_op jit(solution)/shard_map/ppermute | solution.py:41
  155.9 103.1 %reduce-scatter.6.cloned.1.call-start = ((), (), s32[]{:S(2)}) async-start(), calls=%async_computation.8 | async-start | bytes 9437184 | tf_op jit(solution)/shard_map/reduce_scatter | solution.py:75
  156.1 11.1 %copy-start.8 = (bf16[1024,4096]{1,0:T(8,128)(2,1)S(1)}, bf16[1024,4096]{1,0:T(8,128)(2,1)}, u32[]{:S(2)}) copy-start(bf16[1024,4096]{1,0:T(8,128)(2,1)} %all-gather.6.cloned.1.call-done) | copy-start | bytes 25165828
  156.1 21.0 %slice-start = ((s8[6291456]{0:T(1024)(128)(4,1)}), s8[4194304]{0:T(1024)(128)(4,1)S(1)}, s32[]{:S(2)}) async-start(s8[6291456]{0:T(1024)(128)(4,1)} %bitcast.29), calls=%async_computation.10 | async-start | bytes 8388608
  167.2 10.0 %slice-start.1 = ((s8[6291456]{0:T(1024)(128)(4,1)}), s8[2097152]{0:T(1024)(128)(4,1)S(1)}, s32[]{:S(2)}) async-start(s8[6291456]{0:T(1024)(128)(4,1)} %bitcast.29), calls=%async_computation.11 | async-start | bytes 4194304
  186.2 73.4 %copy-start.7 = (f32[128]{0:T(128)S(1)}, f32[128]{0:T(128)}, u32[]{:S(2)}) copy-start(f32[128]{0:T(128)} %param.19) | copy-start | bytes 1540
  186.2 72.8 %copy-start.1 = (bf16[128,4096]{1,0:T(8,128)(2,1)S(1)}, bf16[128,4096]{1,0:T(8,128)(2,1)}, u32[]{:S(2)}) copy-start(bf16[128,4096]{1,0:T(8,128)(2,1)} %all-gather.8.cloned.1.call-done) | copy-start | bytes 3145732
  186.2 102.6 %reduce-scatter.8.cloned.1.call-start = ((), (), s32[]{:S(2)}) async-start(), calls=%async_computation.9 | async-start | bytes 1310720 | tf_op jit(solution)/shard_map/reduce_scatter | solution.py:76
Sparse Core Ops, SparseCore 0:
  9.6 30.6 all-gather.3
  49.8 26.4 reduce-scatter.3
  79.8 76.0 all-gather.5
  157.9 26.5 all-gather.7
  188.2 70.7 reduce-scatter.5
  261.7 27.1 reduce-scatter.7
